TPU v7x, 128 devices: a whole 4x4x4 slice. The times are simulated.
128 devices in a mesh: rows: 8 (over z, core), cols: 16 (over y, x).
Axes of the slice: x: 4, y: 4, z: 4, core: 2. Of those that a mesh axis runs over, the one named last changes fastest.
Arguments:
- pivot_rhs: float32 [4, 4096, 1024], P(None, 'cols'), may hold values from -6 to 6
- bound_sol: bfloat16 [16384, 1024], P('rows'), may hold values from -6 to 6
- border_tiles: bfloat16 [16384, 4, 4096], P('rows', None, 'cols'), may hold values from -0.046875 to 0.046875
- lower_tiles: bfloat16 [6, 4096, 4096], P(None, 'rows', 'cols'), may hold values from -0.09375 to 0.09375
- inverse_diag: bfloat16 [4, 4096, 4096], P(None, 'cols', 'rows'), may hold values from -0.09375 to 0.09375
- owner_map: int32 [128, 128, 1], P(('rows', 'cols')), may hold values from 0 to 127; in each aligned block of 128 rows (0 to 127, 128 to 255, ..., all dimensions but the last counted through in order) at most 2 rows name the same one
Outputs:
- child_rows: float32 [32768, 1024], P(('rows', 'cols'))
Inputs may be any that keep to these rules, and one draw needn't show every extreme that they name: `owner_map`: among the rows of one device (one index of the first dimension), no owner is named more than 2 times, a bound that some block reaches; every owner is named somewhere.
All inputs are finite; a program needn't handle non-finite values.
Results may differ from a plain program's by a relative error of at most 0.008.
Values may be sent and summed in bfloat16 or wider, within the bound.
No kernel may reach another device: no remote copies, remote signals or barrier semaphores. Data moves between devices by JAX's collectives and lax.ppermute only.
A program may use at most 64 MiB of HBM per device.

v0:
```python
import jax
import jax.numpy as jnp
from jax import lax
from jax.sharding import PartitionSpec as P


def pair_slot(later, earlier):
    return later * (later - 1) // 2 + earlier


def pack_rows(rows_here, owners, devices, most):
    onehot = (owners[:, None] == jnp.arange(devices, dtype=jnp.int32)[None, :]).astype(jnp.int32)
    ranks = jnp.cumsum(onehot, axis=0) - onehot
    slots = jnp.sum(ranks * onehot, axis=1)
    target = owners * most + slots
    select = (jnp.arange(devices * most, dtype=jnp.int32)[:, None] == target[None, :]).astype(
        jnp.float32
    )
    return jnp.dot(
        select, rows_here, precision=lax.Precision.HIGHEST, preferred_element_type=jnp.float32
    )


def tile_term(tile, vectors):
    return lax.dot_general(
        tile, vectors, (((0,), (0,)), ((), ())), preferred_element_type=jnp.float32
    )


def local(pivot_rhs, bound_sol, border_tiles, lower_tiles, inverse_diag, owner_map):
    devices = lax.axis_size("rows") * lax.axis_size("cols")
    blocks = pivot_rhs.shape[0]
    width_here = pivot_rhs.shape[1]
    sources = pivot_rhs.shape[2]
    rows_dev = owner_map.shape[1]
    most = max(2, 2 * rows_dev // devices)
    border_part = lax.dot_general(
        border_tiles, bound_sol, (((0,), (0,)), ((), ())), preferred_element_type=jnp.float32
    )
    pending = []
    border_full = lax.psum(border_part, "rows")
    for k in range(blocks):
        pending.append(jnp.zeros((width_here, sources), jnp.float32))
    rounded = [None] * blocks
    own_rows = [None] * blocks
    for k in reversed(range(blocks)):
        local_sum = pending[k]
        for j in range(k + 1, blocks):
            local_sum = local_sum + tile_term(lower_tiles[pair_slot(j, k)], rounded[j])
        summed = lax.psum(local_sum, "rows")
        summed = summed + border_full[k]
        residual = (pivot_rhs[k] - summed).astype(jnp.bfloat16)
        inverse_here = inverse_diag[k]
        solved_here = lax.psum_scatter(
            tile_term(inverse_here, residual), "cols", scatter_dimension=0, tiled=True
        )
        own_rows[k] = solved_here
        if k > 0:
            rounded[k] = lax.all_gather(
                solved_here.astype(jnp.bfloat16), "cols", axis=0, tiled=True
            )
    rows_here = jnp.concatenate(own_rows, axis=0)
    owners = owner_map[0, :, 0]
    buffer = pack_rows(rows_here, owners, devices, most).reshape(devices, most, sources)
    received = lax.all_to_all(buffer, ("rows", "cols"), split_axis=0, concat_axis=0, tiled=True)
    return received.reshape(devices * most, sources)


def solution(mesh):
    placed = (
        P(None, "cols", None),
        P("rows", None),
        P("rows", None, "cols"),
        P(None, "rows", "cols"),
        P(None, "cols", "rows"),
        P(("rows", "cols"), None, None),
    )
    return jax.shard_map(
        local, mesh=mesh, in_specs=placed, out_specs=P(("rows", "cols"), None), check_vma=False
    )
```

profile of v0, /device:TPU:1, one launch (start us, length us, event | category | flops | bytes accessed | tf_op | source)
XLA Modules:
  0.0 773.4 jit_solution(16388644528442897463)
XLA Ops:
  6.5 0.0 all-reduce.5.cloned.1.call-start
  6.5 10.0 %fusion = f32[4,256,1024]{2,1,0:T(8,128)} fusion(bf16[2048,1024]{1,0:T(8,128)(2,1)} %param.7, bf16[2048,4,256]{2,1,0:T(4,128)(2,1)} %param.8), kind=kOutput, calls=%fused_computation | convolution fusion | flops 4294967296 | bytes 12582912 | tf_op jit(solution)/shard_map/dot_general | solution.py:37
  16.6 0.0 all-reduce.5.cloned.1.call-update
  16.6 0.0 reduce-scatter.13.cloned.1.call-start
  16.6 74.5 %all-reduce.5.cloned.1.call-done = f32[4,256,1024]{2,1,0:T(8,128)} async-done(((f32[4,256,1024]{2,1,0:T(8,128)}), f32[4,256,1024]{2,1,0:T(8,128)}) %all-reduce.5.cloned.1.call-update) | async-done | bytes 4194320 | tf_op jit(solution)/shard_map/psum | solution.py:41
  91.2 2.1 convolution_bitcast_fusion.3
  93.2 1.8 copy.28
  95.1 0.0 reduce-scatter.13.cloned.1.call-update
  95.1 0.0 all-gather.4.cloned.1.call-start
  95.1 74.3 %reduce-scatter.13.cloned.1.call-done = f32[32,1024]{1,0:T(8,128)} async-done(((f32[512,1024]{1,0:T(8,128)}), f32[32,1024]{1,0:T(8,128)}) %reduce-scatter.13.cloned.1.call-update) | async-done | bytes 131088 | tf_op jit(solution)/shard_map/reduce_scatter | solution.py:54
  169.5 1.5 convert_element_type.31
  171.0 0.0 all-gather.4.cloned.1.call-update
  171.0 0.0 all-reduce.7.cloned.1.call-start
  171.1 42.9 %all-gather.4.cloned.1.call-done = bf16[512,1024]{1,0:T(8,128)(2,1)} async-done(((bf16[32,1024]{1,0:T(8,128)(2,1)}), bf16[512,1024]{1,0:T(8,128)(2,1)}) %all-gather.4.cloned.1.call-update) | async-done | bytes 1048592 | tf_op jit(solution)/shard_map/all_gather | solution.py:59
  214.0 2.7 convolution_bitcast_fusion.4
  216.7 0.0 all-reduce.7.cloned.1.call-update
  216.7 0.0 reduce-scatter.15.cloned.1.call-start
  216.8 61.5 %all-reduce.7.cloned.1.call-done = f32[256,1024]{1,0:T(8,128)} async-done(((f32[256,1024]{1,0:T(8,128)}), f32[256,1024]{1,0:T(8,128)}) %all-reduce.7.cloned.1.call-update) | async-done | bytes 1048592 | tf_op jit(solution)/shard_map/psum | solution.py:50
  278.3 2.5 convolution_bitcast_fusion.2
  280.8 0.0 copy-start
  280.8 1.8 copy.30
  282.6 0.0 reduce-scatter.15.cloned.1.call-update
  282.6 0.0 all-gather.6.cloned.1.call-start
  282.7 73.8 %reduce-scatter.15.cloned.1.call-done = f32[32,1024]{1,0:T(8,128)} async-done(((f32[512,1024]{1,0:T(8,128)}), f32[32,1024]{1,0:T(8,128)}) %reduce-scatter.15.cloned.1.call-update) | async-done | bytes 131088 | tf_op jit(solution)/shard_map/reduce_scatter | solution.py:54
  356.5 1.5 convert_element_type.33
  358.0 0.0 all-gather.6.cloned.1.call-update
  358.0 0.0 all-reduce.9.cloned.1.call-start
  358.1 42.5 %all-gather.6.cloned.1.call-done = bf16[512,1024]{1,0:T(8,128)(2,1)} async-done(((bf16[32,1024]{1,0:T(8,128)(2,1)}), bf16[512,1024]{1,0:T(8,128)(2,1)}) %all-gather.6.cloned.1.call-update) | async-done | bytes 1048592 | tf_op jit(solution)/shard_map/all_gather | solution.py:59
  400.6 1.7 fusion.35
  402.4 2.4 fusion.4
  404.8 0.0 all-reduce.9.cloned.1.call-update
  404.8 0.0 reduce-scatter.17.cloned.1.call-start
  404.9 61.5 %all-reduce.9.cloned.1.call-done = f32[256,1024]{1,0:T(8,128)} async-done(((f32[256,1024]{1,0:T(8,128)}), f32[256,1024]{1,0:T(8,128)}) %all-reduce.9.cloned.1.call-update) | async-done | bytes 1048592 | tf_op jit(solution)/shard_map/psum | solution.py:50
  466.4 2.5 convolution_bitcast_fusion.1
  468.8 1.8 copy.32
  470.7 0.0 reduce-scatter.17.cloned.1.call-update
  470.7 0.0 all-gather.8.cloned.1.call-start
  470.8 73.8 %reduce-scatter.17.cloned.1.call-done = f32[32,1024]{1,0:T(8,128)} async-done(((f32[512,1024]{1,0:T(8,128)}), f32[32,1024]{1,0:T(8,128)}) %reduce-scatter.17.cloned.1.call-update) | async-done | bytes 131088 | tf_op jit(solution)/shard_map/reduce_scatter | solution.py:54
  544.6 1.5 convert_element_type.35
  546.1 0.0 all-gather.8.cloned.1.call-update
  546.1 0.0 all-reduce.11.cloned.1.call-start
  546.2 42.9 %all-gather.8.cloned.1.call-done = bf16[512,1024]{1,0:T(8,128)(2,1)} async-done(((bf16[32,1024]{1,0:T(8,128)(2,1)}), bf16[512,1024]{1,0:T(8,128)(2,1)}) %all-gather.8.cloned.1.call-update) | async-done | bytes 1048592 | tf_op jit(solution)/shard_map/all_gather | solution.py:59
  589.1 1.7 fusion.31
  590.8 1.4 convolution_add_fusion.1
  592.3 2.4 fusion.3
  594.7 0.0 all-reduce.11.cloned.1.call-update
  594.7 0.2 reduce-scatter.19.cloned.1.call-start
  595.0 61.3 %all-reduce.11.cloned.1.call-done = f32[256,1024]{1,0:T(8,128)} async-done(((f32[256,1024]{1,0:T(8,128)}), f32[256,1024]{1,0:T(8,128)}) %all-reduce.11.cloned.1.call-update) | async-done | bytes 1048592 | tf_op jit(solution)/shard_map/psum | solution.py:50
  656.3 2.5 convolution_bitcast_fusion
  658.8 0.0 copy-start.5
  658.8 1.9 copy.34
  660.7 0.0 reduce-scatter.19.cloned.1.call-update
  660.7 0.1 fusion.51
  660.8 0.2 reduce_window_sum.11
  661.0 0.2 select_reduce_fusion
  661.2 0.2 copy.29
  661.4 0.2 copy.31
  661.6 0.2 copy.33
  661.8 72.8 %reduce-scatter.19.cloned.1.call-done = f32[32,1024]{1,0:T(8,128)} async-done(((f32[512,1024]{1,0:T(8,128)}), f32[32,1024]{1,0:T(8,128)}) %reduce-scatter.19.cloned.1.call-update) | async-done | bytes 131088
  734.6 1.1 copy.35
  735.7 1.0 fusion.20
  736.7 0.6 reshape.16
  737.3 27.9 %all_to_all.5 = f32[128,2,1024]{2,1,0:T(2,128)S(1)} all-to-all(f32[128,2,1024]{2,1,0:T(2,128)S(1)} %reshape.16), channel_id=1, replica_groups=mesh['rows'=8,'cols'=16] {'rows','cols'}, dimensions={0} | all-to-all | bytes 2097152 | tf_op jit(solution)/shard_map/all_to_all | solution.py:65
  765.2 1.7 reshape.17
  (11 shorter events, 0.0 us)
Async XLA Ops:
  6.5 84.6 %all-reduce.5.cloned.1.call-start = ((), (), s32[]{:S(2)}) async-start(), calls=%async_computation.5 | async-start | bytes 8388608 | tf_op jit(solution)/shard_map/psum | solution.py:41
  16.6 152.9 %reduce-scatter.13.cloned.1.call-start = ((), (), s32[]{:S(2)}) async-start(), calls=%async_computation.12 | async-start | bytes 2228224 | tf_op jit(solution)/shard_map/reduce_scatter | solution.py:54
  95.1 118.9 %all-gather.4.cloned.1.call-start = ((), (), s32[]{:S(2)}) async-start(), calls=%async_computation.6 | async-start | bytes 1114112 | tf_op jit(solution)/shard_map/all_gather | solution.py:59
  171.0 107.3 %all-reduce.7.cloned.1.call-start = ((), (), s32[]{:S(2)}) async-start(), calls=%async_computation.7 | async-start | bytes 2097152 | tf_op jit(solution)/shard_map/psum | solution.py:50
  216.7 139.7 %reduce-scatter.15.cloned.1.call-start = ((), (), s32[]{:S(2)}) async-start(), calls=%async_computation.13 | async-start | bytes 2228224 | tf_op jit(solution)/shard_map/reduce_scatter | solution.py:54
  280.8 121.6 %copy-start = (bf16[512,1024]{1,0:T(8,128)(2,1)S(1)}, bf16[512,1024]{1,0:T(8,128)(2,1)}, u32[]{:S(2)}) copy-start(bf16[512,1024]{1,0:T(8,128)(2,1)} %all-gather.4.cloned.1.call-done) | copy-start | bytes 3145732
  282.6 118.0 %all-gather.6.cloned.1.call-start = ((), (), s32[]{:S(2)}) async-start(), calls=%async_computation.8 | async-start | bytes 1114112 | tf_op jit(solution)/shard_map/all_gather | solution.py:59
  358.0 108.3 %all-reduce.9.cloned.1.call-start = ((), (), s32[]{:S(2)}) async-start(), calls=%async_computation.9 | async-start | bytes 2097152 | tf_op jit(solution)/shard_map/psum | solution.py:50
  404.8 139.7 %reduce-scatter.17.cloned.1.call-start = ((), (), s32[]{:S(2)}) async-start(), calls=%async_computation.14 | async-start | bytes 2228224 | tf_op jit(solution)/shard_map/reduce_scatter | solution.py:54
  470.7 120.1 %copy-start.1 = (bf16[512,1024]{1,0:T(8,128)(2,1)S(1)}, bf16[512,1024]{1,0:T(8,128)(2,1)}, u32[]{:S(2)}) copy-start(bf16[512,1024]{1,0:T(8,128)(2,1)} %all-gather.6.cloned.1.call-done) | copy-start | bytes 3145732
  470.7 118.4 %all-gather.8.cloned.1.call-start = ((), (), s32[]{:S(2)}) async-start(), calls=%async_computation.10 | async-start | bytes 1114112 | tf_op jit(solution)/shard_map/all_gather | solution.py:59
  546.1 110.1 %all-reduce.11.cloned.1.call-start = ((), (), s32[]{:S(2)}) async-start(), calls=%async_computation.11 | async-start | bytes 2097152 | tf_op jit(solution)/shard_map/psum | solution.py:50
  594.7 139.9 %reduce-scatter.19.cloned.1.call-start = ((), (), s32[]{:S(2)}) async-start(), calls=%async_computation.15 | async-start | bytes 2228224
  658.8 1.9 copy-start.5
  658.8 2.4 copy-start.2
  658.8 2.6 copy-start.3
  658.8 2.8 copy-start.4
Sparse Core Ops, SparseCore 0:
  16.7 74.4 all-reduce.4
  95.2 74.1 reduce-scatter.12
  171.8 42.1 all-gather.3
  216.9 61.3 all-reduce.6
  282.8 73.6 reduce-scatter.14
  358.5 42.1 all-gather.5
  404.9 61.3 all-reduce.8
  470.8 73.6 reduce-scatter.16
  546.9 42.0 all-gather.7
  594.8 61.3 all-reduce.10
  660.8 73.7 reduce-scatter.18
where the time goes:
time: 774 us; the launch traced here: 773 us
  waiting for transfers between devices  682 us (88%)
  matrix products  33 us (4%)
  blocking collectives  27.9 us (4%)
  between operations  13.4 us (2%)
  local copies, waits for them, and re-layouts  11.4 us (1%)
    reduce_scatter x3, waiting for transfers between devices, local(): lax.psum_scatter(tile_term(inverse_here, residual), 'cols', scatter_dimen...  222 us
    psum x3, waiting for transfers between devices, local(): summed = lax.psum(local_sum, 'rows')  184 us
    all_gather x3, waiting for transfers between devices, local(): lax.all_gather(solved_here.astype(jnp.bfloat16), 'cols', axis=0, tiled=True)  128 us
    psum x1, waiting for transfers between devices, local(): border_full = lax.psum(border_part, 'rows')  74.5 us
    unnamed x12, waiting for transfers between devices  73 us
    all_to_all x1, blocking collectives, local(): lax.all_to_all(buffer, ('rows', 'cols'), split_axis=0, concat_axis=0, til...  27.9 us
    dot_general x10, matrix products, tile_term(): lax.dot_general(tile, vectors, (((0,), (0,)), ((), ())), preferred_elemen...  22 us
  transfers between devices with their start and end apart: 11, of which 11 were waited for; matrix products, arithmetic and copies ran while one was open for 0% of the time, Pallas kernels for 0%

commit v1 on v0

--- a/solution.py
+++ b/solution.py
@@ -2,6 +2,28 @@
 import jax.numpy as jnp
 from jax import lax
 from jax.sharding import PartitionSpec as P
+
+
+def joined_along(pieces, dim):
+    shape = list(pieces.shape[1:])
+    shape[dim] *= pieces.shape[0]
+    return jnp.moveaxis(pieces, 0, dim).reshape(shape)
+
+
+def ring_gather(x, axis, dim):
+    size = lax.axis_size(axis)
+    pairs = [(i, (i + 1) % size) for i in range(size)]
+    back = [(b, a) for a, b in pairs]
+    lower, upper = ([], [])
+    for lap in range(size - 1):
+        if lap % 2 == 0:
+            lower.append(lax.ppermute(lower[-1] if lower else x, axis, pairs))
+        else:
+            upper.append(lax.ppermute(upper[-1] if upper else x, axis, back))
+    parts = jnp.stack([*lower[::-1], x, *upper])
+    shift = lax.axis_index(axis) - len(lower)
+    parts = parts[(jnp.arange(size) - shift) % size]
+    return joined_along(parts, dim)
 
 
 def pair_slot(later, earlier):
@@ -56,9 +78,7 @@
         )
         own_rows[k] = solved_here
         if k > 0:
-            rounded[k] = lax.all_gather(
-                solved_here.astype(jnp.bfloat16), "cols", axis=0, tiled=True
-            )
+            rounded[k] = ring_gather(solved_here.astype(jnp.bfloat16), "cols", 0)
     rows_here = jnp.concatenate(own_rows, axis=0)
     owners = owner_map[0, :, 0]
     buffer = pack_rows(rows_here, owners, devices, most).reshape(devices, most, sources)

time: 774 us -> 939 us (1.21)
  starting transfers between devices: 0.6 us -> 113 us
  local copies, waits for them, and re-layouts: 11.4 us -> 65.8 us
    reduce_scatter x3 -> x0, waiting for transfers between devices: 222 us -> none  [local(): lax.psum_scatter(tile_term(inverse_here, residual), 'cols', scatter_dimen...]
    unnamed x12, waiting for transfers between devices: 73 us -> 286 us
    all_gather x3 -> x0, waiting for transfers between devices: 128 us -> none  [local(): lax.all_gather(solved_here.astype(jnp.bfloat16), 'cols', axis=0, tiled=True)]
    ppermute x0 -> x45, starting transfers between devices: none -> 104 us  [the longest x21 101 us: ring_gather(): upper.append(lax.ppermute(upper[-1] if upper else x, axis, back))]
    ppermute x0 -> x45, waiting for transfers between devices: none -> 98.9 us  [the longest x24 98.5 us: ring_gather(): lower.append(lax.ppermute(lower[-1] if lower else x, axis, pairs))]
    another operation x0 -> x51, local copies, waits for them, and re-layouts: none -> 34.3 us  [ring_gather(): parts = jnp.stack([*lower[::-1], x, *upper])]
    psum x3, waiting for transfers between devices: 184 us -> 214 us  [local(): summed = lax.psum(local_sum, 'rows')]
    unnamed x20 -> x95, local copies, waits for them, and re-layouts: 9.1 us -> 26.1 us
  transfers between devices with their start and end apart: 11 -> 53, of which waited for: 11 -> 34; matrix products, arithmetic and copies ran while one was open for 0% -> 3% of each run, Pallas kernels for 0% -> 0%
where the time goes in v1:
time: 939 us; the launch traced here: 930 us
  waiting for transfers between devices  674 us (72%)
  starting transfers between devices  113 us (12%)
  local copies, waits for them, and re-layouts  65.8 us (7%)
  matrix products  34.5 us (4%)
  blocking collectives  27.9 us (3%)
  between operations  14.4 us (2%)
    unnamed x12, waiting for transfers between devices  286 us
    psum x3, waiting for transfers between devices, local(): summed = lax.psum(local_sum, 'rows')  214 us
    ppermute x21, starting transfers between devices, ring_gather(): upper.append(lax.ppermute(upper[-1] if upper else x, axis, back))  101 us
    ppermute x24, waiting for transfers between devices, ring_gather(): lower.append(lax.ppermute(lower[-1] if lower else x, axis, pairs))  98.5 us
    psum x1, waiting for transfers between devices, local(): border_full = lax.psum(border_part, 'rows')  74.5 us
    another operation x51, local copies, waits for them, and re-layouts, ring_gather(): parts = jnp.stack([*lower[::-1], x, *upper])  34.3 us
    all_to_all x1, blocking collectives, local(): lax.all_to_all(buffer, ('rows', 'cols'), split_axis=0, concat_axis=0, til...  27.9 us
    unnamed x95, local copies, waits for them, and re-layouts  26.1 us
  transfers between devices with their start and end apart: 53, of which 34 were waited for; matrix products, arithmetic and copies ran while one was open for 3% of the time, Pallas kernels for 0%

profile of v1, /device:TPU:1, one launch (start us, length us, event | category | flops | bytes accessed | tf_op | source)
XLA Modules:
  0.0 930.0 jit_solution(9254737905798921465)
XLA Ops:
  6.5 10.0 %fusion = f32[4,256,1024]{2,1,0:T(8,128)} fusion(bf16[2048,1024]{1,0:T(8,128)(2,1)} %param.7, bf16[2048,4,256]{2,1,0:T(4,128)(2,1)} %param.8), kind=kOutput, calls=%fused_computation.3 | convolution fusion | flops 4294967296 | bytes 12582912 | tf_op jit(solution)/shard_map/dot_general | solution.py:59
  16.6 74.5 %all-reduce.5.cloned.1.call-done = f32[4,256,1024]{2,1,0:T(8,128)} async-done(((f32[4,256,1024]{2,1,0:T(8,128)}), f32[4,256,1024]{2,1,0:T(8,128)}) %all-reduce.5.cloned.1.call-update) | async-done | bytes 4194320 | tf_op jit(solution)/shard_map/psum | solution.py:63
  91.2 2.1 convolution_bitcast_fusion.3
  93.2 1.9 copy.73
  95.2 74.3 %reduce-scatter.13.cloned.1.call-done = f32[32,1024]{1,0:T(8,128)} async-done(((f32[512,1024]{1,0:T(8,128)}), f32[32,1024]{1,0:T(8,128)}) %reduce-scatter.13.cloned.1.call-update) | async-done | bytes 131088
  171.2 4.3 collective-permute-start.8
  175.5 3.8 collective-permute-done
  179.2 4.8 collective-permute-start.9
  184.0 3.8 collective-permute-done.1
  187.8 4.8 collective-permute-start.10
  192.6 3.8 collective-permute-done.2
  196.3 4.8 collective-permute-start.11
  201.1 3.8 collective-permute-done.3
  204.9 4.8 collective-permute-start.12
  209.6 4.3 collective-permute-done.4
  213.9 5.0 collective-permute-start.13
  219.0 5.1 collective-permute-done.5
  224.2 5.3 collective-permute-start.14
  229.5 6.0 collective-permute-done.6
  241.5 6.0 collective-permute-done.7
  249.4 2.4 convolution_bitcast_fusion.4
  251.9 68.0 %all-reduce.7.cloned.1.call-done = f32[256,1024]{1,0:T(8,128)} async-done(((f32[256,1024]{1,0:T(8,128)}), f32[256,1024]{1,0:T(8,128)}) %all-reduce.7.cloned.1.call-update) | async-done | bytes 1048592 | tf_op jit(solution)/shard_map/psum | solution.py:72
  319.9 2.5 convolution_bitcast_fusion.2
  324.3 73.8 %reduce-scatter.15.cloned.1.call-done = f32[32,1024]{1,0:T(8,128)} async-done(((f32[512,1024]{1,0:T(8,128)}), f32[32,1024]{1,0:T(8,128)}) %reduce-scatter.15.cloned.1.call-update) | async-done | bytes 131088
  399.8 4.3 collective-permute-start.23
  404.1 3.8 collective-permute-done.15
  407.9 4.8 collective-permute-start.24
  412.7 3.8 collective-permute-done.16
  416.4 4.8 collective-permute-start.25
  421.2 3.8 collective-permute-done.17
  425.0 4.8 collective-permute-start.26
  429.7 3.8 collective-permute-done.18
  433.5 4.8 collective-permute-start.27
  438.3 4.3 collective-permute-done.19
  442.6 5.1 collective-permute-start.28
  447.6 5.1 collective-permute-done.20
  452.8 5.3 collective-permute-start.29
  458.2 6.0 collective-permute-done.21
  481.4 2.4 fusion.4
  483.9 72.3 %all-reduce.9.cloned.1.call-done = f32[256,1024]{1,0:T(8,128)} async-done(((f32[256,1024]{1,0:T(8,128)}), f32[256,1024]{1,0:T(8,128)}) %all-reduce.9.cloned.1.call-update) | async-done | bytes 1048592 | tf_op jit(solution)/shard_map/psum | solution.py:72
  556.2 3.9 convolution_bitcast_fusion.1
  560.1 3.0 copy.77
  563.0 9.3 %all-reduce.11.cloned.1.call-start = ((), (), s32[]{:S(2)}) async-start(), calls=%async_computation.8 | async-start | bytes 2097152 | tf_op jit(solution)/shard_map/psum | solution.py:72
  572.4 64.5 %reduce-scatter.17.cloned.1.call-done = f32[32,1024]{1,0:T(8,128)} async-done(((f32[512,1024]{1,0:T(8,128)}), f32[32,1024]{1,0:T(8,128)}) %reduce-scatter.17.cloned.1.call-update) | async-done | bytes 131088
  638.7 4.3 collective-permute-start.38
  642.9 3.8 collective-permute-done.30
  646.7 4.8 collective-permute-start.39
  651.5 3.8 collective-permute-done.31
  655.3 4.8 collective-permute-start.40
  660.0 3.8 collective-permute-done.32
  663.8 4.8 collective-permute-start.41
  668.6 3.8 collective-permute-done.33
  672.3 4.8 collective-permute-start.42
  677.1 4.3 collective-permute-done.34
  681.4 5.1 collective-permute-start.43
  686.5 5.1 collective-permute-done.35
  691.7 5.3 collective-permute-start.44
  697.0 6.0 collective-permute-done.36
  735.2 2.4 fusion.3
  737.7 73.8 %all-reduce.11.cloned.1.call-done = f32[256,1024]{1,0:T(8,128)} async-done(((f32[256,1024]{1,0:T(8,128)}), f32[256,1024]{1,0:T(8,128)}) %all-reduce.11.cloned.1.call-update) | async-done | bytes 1048592 | tf_op jit(solution)/shard_map/psum | solution.py:72
  811.5 2.5 convolution_bitcast_fusion
  816.4 73.5 %reduce-scatter.19.cloned.1.call-done = f32[32,1024]{1,0:T(8,128)} async-done(((f32[512,1024]{1,0:T(8,128)}), f32[32,1024]{1,0:T(8,128)}) %reduce-scatter.19.cloned.1.call-update) | async-done | bytes 131088
  891.0 2.0 fusion.20
  893.6 27.9 %all_to_all.5 = f32[128,2,1024]{2,1,0:T(2,128)S(1)} all-to-all(f32[128,2,1024]{2,1,0:T(2,128)S(1)} %reshape.77), channel_id=1, replica_groups=mesh['rows'=8,'cols'=16] {'rows','cols'}, dimensions={0} | all-to-all | bytes 2097152 | tf_op jit(solution)/shard_map/all_to_all | solution.py:85
  (226 shorter events, 70.3 us)
Async XLA Ops:
  6.5 84.6 %all-reduce.5.cloned.1.call-start = ((), (), s32[]{:S(2)}) async-start(), calls=%async_computation.5 | async-start | bytes 8388608 | tf_op jit(solution)/shard_map/psum | solution.py:63
  16.6 152.9 %reduce-scatter.13.cloned.1.call-start = ((), (), s32[]{:S(2)}) async-start(), calls=%async_computation.9 | async-start | bytes 2228224
  95.1 224.7 %all-reduce.7.cloned.1.call-start = ((), (), s32[]{:S(2)}) async-start(), calls=%async_computation.6 | async-start | bytes 2097152 | tf_op jit(solution)/shard_map/psum | solution.py:72
  170.6 78.2 %copy-start = (f32[32,1024]{0,1:T(8,128)}, f32[32,1024]{0,1:T(8,128)S(1)}, u32[]{:S(2)}) copy-start(f32[32,1024]{0,1:T(8,128)S(1)} %copy.74) | copy-start | bytes 393220
  170.6 8.6 collective-permute-start
  171.2 8.0 collective-permute-start.8
  179.2 8.5 collective-permute-start.1
  179.2 8.5 collective-permute-start.9
  187.8 8.5 collective-permute-start.2
  187.8 8.5 collective-permute-start.10
  196.3 8.5 collective-permute-start.3
  196.3 8.5 collective-permute-start.11
  204.8 9.1 collective-permute-start.4
  204.9 9.1 collective-permute-start.12
  213.9 10.1 %collective-permute-start.5 = (bf16[32,1024]{0,1:T(8,128)(2,1)S(1)}, bf16[32,1024]{0,1:T(8,128)(2,1)S(1)}, u32[]{:S(2)}, u32[]{:S(2)}) collective-permute-start(bf16[32,1024]{0,1:T(8,128)(2,1)S(1)} %collective-permute-done.4), channel_id=1, source_target_pairs={{0,1},{1,2},{2,3},{3,4},{4,5},{5,6},{6,7},{7,8},{8,9},{9,10},{10,1... | collective-permute-start | bytes 196616 | tf_op jit(solution)/shard_map/ppermute | solution.py:20
  213.9 10.2 %collective-permute-start.13 = (bf16[32,1024]{0,1:T(8,128)(2,1)S(1)}, bf16[32,1024]{0,1:T(8,128)(2,1)}, u32[]{:S(2)}, u32[]{:S(2)}) collective-permute-start(bf16[32,1024]{0,1:T(8,128)(2,1)S(1)} %collective-permute-done.12), channel_id=1, source_target_pairs={{1,0},{2,1},{3,2},{4,3},{5,4},{6,5},{7,6},{8,7},{9,8},{10,9},{11,1... | collective-permute-start | bytes 196616 | tf_op jit(solution)/shard_map/ppermute | solution.py:22
  224.1 11.5 %collective-permute-start.6 = (bf16[32,1024]{0,1:T(8,128)(2,1)S(1)}, bf16[32,1024]{0,1:T(8,128)(2,1)}, u32[]{:S(2)}, u32[]{:S(2)}) collective-permute-start(bf16[32,1024]{0,1:T(8,128)(2,1)S(1)} %collective-permute-done.5), channel_id=1, source_target_pairs={{0,1},{1,2},{2,3},{3,4},{4,5},{5,6},{6,7},{7,8},{8,9},{9,10},{10,1... | collective-permute-start | bytes 196616 | tf_op jit(solution)/shard_map/ppermute | solution.py:20
  224.2 15.2 %collective-permute-start.14 = (bf16[32,1024]{0,1:T(8,128)(2,1)}, bf16[32,1024]{0,1:T(8,128)(2,1)}, u32[]{:S(2)}, u32[]{:S(2)}) collective-permute-start(bf16[32,1024]{0,1:T(8,128)(2,1)} %collective-permute-done.13), channel_id=1, source_target_pairs={{1,0},{2,1},{3,2},{4,3},{5,4},{6,5},{7,6},{8,7},{9,8},{10,9},{11,1... | collective-permute-start | bytes 196616 | tf_op jit(solution)/shard_map/ppermute | solution.py:22
  235.5 11.9 %collective-permute-start.7 = (bf16[32,1024]{0,1:T(8,128)(2,1)}, bf16[32,1024]{0,1:T(8,128)(2,1)}, u32[]{:S(2)}, u32[]{:S(2)}) collective-permute-start(bf16[32,1024]{0,1:T(8,128)(2,1)} %collective-permute-done.6), channel_id=1, source_target_pairs={{0,1},{1,2},{2,3},{3,4},{4,5},{5,6},{6,7},{7,8},{8,9},{9,10},{10,1... | collective-permute-start | bytes 196616 | tf_op jit(solution)/shard_map/ppermute | solution.py:20
  251.9 146.3 %reduce-scatter.15.cloned.1.call-start = ((), (), s32[]{:S(2)}) async-start(), calls=%async_computation.10 | async-start | bytes 2228224
  324.2 232.0 %all-reduce.9.cloned.1.call-start = ((), (), s32[]{:S(2)}) async-start(), calls=%async_computation.7 | async-start | bytes 2097152 | tf_op jit(solution)/shard_map/psum | solution.py:72
  399.2 80.1 %copy-start.2 = (f32[32,1024]{0,1:T(8,128)}, f32[32,1024]{0,1:T(8,128)S(1)}, u32[]{:S(2)}) copy-start(f32[32,1024]{0,1:T(8,128)S(1)} %copy.76) | copy-start | bytes 393220
  399.3 8.6 collective-permute-start.15
  399.8 8.1 collective-permute-start.23
  407.9 8.5 collective-permute-start.16
  407.9 8.5 collective-permute-start.24
  416.4 8.5 collective-permute-start.17
  416.4 8.5 collective-permute-start.25
  425.0 8.5 collective-permute-start.18
  425.0 8.5 collective-permute-start.26
  433.5 9.1 collective-permute-start.19
  433.5 9.1 collective-permute-start.27
  442.6 10.1 %collective-permute-start.20 = (bf16[32,1024]{0,1:T(8,128)(2,1)S(1)}, bf16[32,1024]{0,1:T(8,128)(2,1)S(1)}, u32[]{:S(2)}, u32[]{:S(2)}) collective-permute-start(bf16[32,1024]{0,1:T(8,128)(2,1)S(1)} %collective-permute-done.19), channel_id=1, source_target_pairs={{0,1},{1,2},{2,3},{3,4},{4,5},{5,6},{6,7},{7,8},{8,9},{9,10},{10,1... | collective-permute-start | bytes 196616 | tf_op jit(solution)/shard_map/ppermute | solution.py:20
  442.6 10.2 %collective-permute-start.28 = (bf16[32,1024]{0,1:T(8,128)(2,1)S(1)}, bf16[32,1024]{0,1:T(8,128)(2,1)}, u32[]{:S(2)}, u32[]{:S(2)}) collective-permute-start(bf16[32,1024]{0,1:T(8,128)(2,1)S(1)} %collective-permute-done.27), channel_id=1, source_target_pairs={{1,0},{2,1},{3,2},{4,3},{5,4},{6,5},{7,6},{8,7},{9,8},{10,9},{11,1... | collective-permute-start | bytes 196616 | tf_op jit(solution)/shard_map/ppermute | solution.py:22
  452.7 11.5 %collective-permute-start.21 = (bf16[32,1024]{0,1:T(8,128)(2,1)S(1)}, bf16[32,1024]{0,1:T(8,128)(2,1)}, u32[]{:S(2)}, u32[]{:S(2)}) collective-permute-start(bf16[32,1024]{0,1:T(8,128)(2,1)S(1)} %collective-permute-done.20), channel_id=1, source_target_pairs={{0,1},{1,2},{2,3},{3,4},{4,5},{5,6},{6,7},{7,8},{8,9},{9,10},{10,1... | collective-permute-start | bytes 196616 | tf_op jit(solution)/shard_map/ppermute | solution.py:20
  452.8 18.8 %collective-permute-start.29 = (bf16[32,1024]{0,1:T(8,128)(2,1)}, bf16[32,1024]{0,1:T(8,128)(2,1)}, u32[]{:S(2)}, u32[]{:S(2)}) collective-permute-start(bf16[32,1024]{0,1:T(8,128)(2,1)} %collective-permute-done.28), channel_id=1, source_target_pairs={{1,0},{2,1},{3,2},{4,3},{5,4},{6,5},{7,6},{8,7},{9,8},{10,9},{11,1... | collective-permute-start | bytes 196616 | tf_op jit(solution)/shard_map/ppermute | solution.py:22
  464.2 11.5 %collective-permute-start.22 = (bf16[32,1024]{0,1:T(8,128)(2,1)}, bf16[32,1024]{0,1:T(8,128)(2,1)}, u32[]{:S(2)}, u32[]{:S(2)}) collective-permute-start(bf16[32,1024]{0,1:T(8,128)(2,1)} %collective-permute-done.21), channel_id=1, source_target_pairs={{0,1},{1,2},{2,3},{3,4},{4,5},{5,6},{6,7},{7,8},{8,9},{9,10},{10,1... | collective-permute-start | bytes 196616 | tf_op jit(solution)/shard_map/ppermute | solution.py:20
  483.8 153.1 %reduce-scatter.17.cloned.1.call-start = ((), (), s32[]{:S(2)}) async-start(), calls=%async_computation.11 | async-start | bytes 2228224
  563.0 248.5 %all-reduce.11.cloned.1.call-start = ((), (), s32[]{:S(2)}) async-start(), calls=%async_computation.8 | async-start | bytes 2097152 | tf_op jit(solution)/shard_map/psum | solution.py:72
  638.0 89.9 %copy-start.4 = (f32[32,1024]{0,1:T(8,128)}, f32[32,1024]{0,1:T(8,128)S(1)}, u32[]{:S(2)}) copy-start(f32[32,1024]{0,1:T(8,128)S(1)} %copy.78) | copy-start | bytes 393220
  638.1 8.6 collective-permute-start.30
  638.7 8.0 collective-permute-start.38
  646.7 8.5 collective-permute-start.31
  646.7 8.5 collective-permute-start.39
  655.2 47.8 %copy-start.5 = (bf16[32,1024]{0,1:T(8,128)(2,1)}, bf16[32,1024]{0,1:T(8,128)(2,1)S(1)}, u32[]{:S(2)}) copy-start(bf16[32,1024]{0,1:T(8,128)(2,1)S(1)} %collective-permute-done.31) | copy-start | bytes 196612
  655.2 8.5 collective-permute-start.32
  655.2 47.8 %copy-start.6 = (bf16[32,1024]{0,1:T(8,128)(2,1)}, bf16[32,1024]{0,1:T(8,128)(2,1)S(1)}, u32[]{:S(2)}) copy-start(bf16[32,1024]{0,1:T(8,128)(2,1)S(1)} %collective-permute-done.39) | copy-start | bytes 196612
  655.3 8.5 collective-permute-start.40
  663.8 39.2 %copy-start.7 = (bf16[32,1024]{0,1:T(8,128)(2,1)}, bf16[32,1024]{0,1:T(8,128)(2,1)S(1)}, u32[]{:S(2)}) copy-start(bf16[32,1024]{0,1:T(8,128)(2,1)S(1)} %collective-permute-done.32) | copy-start | bytes 196612
  663.8 8.5 collective-permute-start.33
  663.8 39.2 %copy-start.8 = (bf16[32,1024]{0,1:T(8,128)(2,1)}, bf16[32,1024]{0,1:T(8,128)(2,1)S(1)}, u32[]{:S(2)}) copy-start(bf16[32,1024]{0,1:T(8,128)(2,1)S(1)} %collective-permute-done.40) | copy-start | bytes 196612
  663.8 8.5 collective-permute-start.41
  672.3 30.7 %copy-start.10 = (bf16[32,1024]{0,1:T(8,128)(2,1)}, bf16[32,1024]{0,1:T(8,128)(2,1)S(1)}, u32[]{:S(2)}) copy-start(bf16[32,1024]{0,1:T(8,128)(2,1)S(1)} %collective-permute-done.33) | copy-start | bytes 196612
  672.3 9.1 collective-permute-start.34
  672.3 30.7 %copy-start.12 = (bf16[32,1024]{0,1:T(8,128)(2,1)}, bf16[32,1024]{0,1:T(8,128)(2,1)S(1)}, u32[]{:S(2)}) copy-start(bf16[32,1024]{0,1:T(8,128)(2,1)S(1)} %collective-permute-done.41) | copy-start | bytes 196612
  672.3 9.1 collective-permute-start.42
  681.4 10.1 %collective-permute-start.35 = (bf16[32,1024]{0,1:T(8,128)(2,1)S(1)}, bf16[32,1024]{0,1:T(8,128)(2,1)S(1)}, u32[]{:S(2)}, u32[]{:S(2)}) collective-permute-start(bf16[32,1024]{0,1:T(8,128)(2,1)S(1)} %collective-permute-done.34), channel_id=1, source_target_pairs={{0,1},{1,2},{2,3},{3,4},{4,5},{5,6},{6,7},{7,8},{8,9},{9,10},{10,1... | collective-permute-start | bytes 196616 | tf_op jit(solution)/shard_map/ppermute | solution.py:20
  681.4 10.2 %collective-permute-start.43 = (bf16[32,1024]{0,1:T(8,128)(2,1)S(1)}, bf16[32,1024]{0,1:T(8,128)(2,1)}, u32[]{:S(2)}, u32[]{:S(2)}) collective-permute-start(bf16[32,1024]{0,1:T(8,128)(2,1)S(1)} %collective-permute-done.42), channel_id=1, source_target_pairs={{1,0},{2,1},{3,2},{4,3},{5,4},{6,5},{7,6},{8,7},{9,8},{10,9},{11,1... | collective-permute-start | bytes 196616 | tf_op jit(solution)/shard_map/ppermute | solution.py:22
  691.5 11.5 %collective-permute-start.36 = (bf16[32,1024]{0,1:T(8,128)(2,1)S(1)}, bf16[32,1024]{0,1:T(8,128)(2,1)}, u32[]{:S(2)}, u32[]{:S(2)}) collective-permute-start(bf16[32,1024]{0,1:T(8,128)(2,1)S(1)} %collective-permute-done.35), channel_id=1, source_target_pairs={{0,1},{1,2},{2,3},{3,4},{4,5},{5,6},{6,7},{7,8},{8,9},{9,10},{10,1... | collective-permute-start | bytes 196616 | tf_op jit(solution)/shard_map/ppermute | solution.py:20
  691.7 22.6 %collective-permute-start.44 = (bf16[32,1024]{0,1:T(8,128)(2,1)}, bf16[32,1024]{0,1:T(8,128)(2,1)}, u32[]{:S(2)}, u32[]{:S(2)}) collective-permute-start(bf16[32,1024]{0,1:T(8,128)(2,1)} %collective-permute-done.43), channel_id=1, source_target_pairs={{1,0},{2,1},{3,2},{4,3},{5,4},{6,5},{7,6},{8,7},{9,8},{10,9},{11,1... | collective-permute-start | bytes 196616 | tf_op jit(solution)/shard_map/ppermute | solution.py:22
  703.1 13.9 %collective-permute-start.37 = (bf16[32,1024]{0,1:T(8,128)(2,1)}, bf16[32,1024]{0,1:T(8,128)(2,1)}, u32[]{:S(2)}, u32[]{:S(2)}) collective-permute-start(bf16[32,1024]{0,1:T(8,128)(2,1)} %collective-permute-done.36), channel_id=1, source_target_pairs={{0,1},{1,2},{2,3},{3,4},{4,5},{5,6},{6,7},{7,8},{8,9},{9,10},{10,1... | collective-permute-start | bytes 196616 | tf_op jit(solution)/shard_map/ppermute | solution.py:20
  737.7 152.2 %reduce-scatter.19.cloned.1.call-start = ((), (), s32[]{:S(2)}) async-start(), calls=%async_computation.12 | async-start | bytes 2228224
  814.0 77.0 %copy-start.1 = (f32[32,1024]{0,1:T(8,128)S(1)}, f32[32,1024]{0,1:T(8,128)}, u32[]{:S(2)}) copy-start(f32[32,1024]{0,1:T(8,128)} %copy-done) | copy-start | bytes 393220
  814.0 77.0 %copy-start.3 = (f32[32,1024]{0,1:T(8,128)S(1)}, f32[32,1024]{0,1:T(8,128)}, u32[]{:S(2)}) copy-start(f32[32,1024]{0,1:T(8,128)} %copy-done.2) | copy-start | bytes 393220
  (10 other events, 184.3 us)
Sparse Core Ops, SparseCore 0:
  16.7 74.4 all-reduce.4
  95.2 74.1 reduce-scatter.12
  252.0 67.8 all-reduce.6
  324.3 73.7 reduce-scatter.14
  484.0 72.1 all-reduce.8
  563.2 73.7 reduce-scatter.16
  737.8 73.6 all-reduce.10
  816.0 73.7 reduce-scatter.18
